TPU v7x, 32 devices: a whole 2x2x4 slice. The times are simulated.
32 devices in a mesh: dp: 4 (over y, x), expert: 8 (over z, core).
Axes of the slice: x: 2, y: 2, z: 4, core: 2. Of those that a mesh axis runs over, the one named last changes fastest.
Arguments:
- tokens: bfloat16 [32768, 768], P(('dp', 'expert')), may hold values from -6 to 6
- cotangent: bfloat16 [32768, 768], P(('dp', 'expert')), may hold values from -6 to 6
- seg_start: int32 [32768], P(('dp', 'expert')), may hold values from 0 to 1023, as said below
- dispatch_slot: int32 [32768], P(('dp', 'expert')), may hold values from 0 to 2048, as said below
- ln1_gain: float32 [768], replicated, may hold values from 0.25 to 1.75
- ln1_shift: float32 [768], replicated, may hold values from -3 to 3
- w_qkv: bfloat16 [768, 2304], replicated, may hold values from -0.21875 to 0.21875
- w_attn_out: bfloat16 [768, 768], replicated, may hold values from -0.875 to 0.875
- ln2_gain: float32 [768], replicated, may hold values from 0.25 to 1.75
- ln2_shift: float32 [768], replicated, may hold values from -3 to 3
- w_in: bfloat16 [2, 768, 3072], replicated, may hold values from -0.21875 to 0.21875
- w_out: bfloat16 [2, 3072, 768], replicated, may hold values from -0.109375 to 0.109375
Outputs:
- result_out: bfloat16 [32768, 768], P(('dp', 'expert'))
- grad_tokens: float32 [32768, 768], P(('dp', 'expert'))
- grad_ln1_gain: float32 [768], replicated
- grad_ln1_shift: float32 [768], replicated
- grad_w_qkv: float32 [768, 2304], replicated
- grad_w_attn_out: float32 [768, 768], replicated
- grad_ln2_gain: float32 [768], replicated
- grad_ln2_shift: float32 [768], replicated
- grad_w_in: float32 [2, 768, 3072], P(None, None, 'expert')
- grad_w_out: float32 [2, 3072, 768], P(None, 'expert')
- expert_counts: int32 [2], replicated
Inputs may be any that keep to these rules, and one draw needn't show every extreme that they name: A row is an image row or a caption row. An image row's first 985 slots hold 5 images of 197 patches each, its other slots are padding, each padding token a segment of its own; a caption row is filled with captions. A token attends only to tokens of its own row with the same seg_start. `dispatch_slot`: slot s sends the token to the device at expert index s // 256 of its dp index, at place s % 256. Image tokens go to expert indices below 4, caption tokens to the others; no two tokens of one device share a slot; padding tokens, and only they, have s = 2048.
All inputs are finite; a program needn't handle non-finite values.
Results may differ from a plain program's by a relative error of at most 0.012.
Values may be sent and summed in bfloat16 or wider, within the bound.
No kernel may reach another device: no remote copies, remote signals or barrier semaphores. Data moves between devices by JAX's collectives and lax.ppermute only.
A program may use at most 320 MiB of HBM per device.

v0:
```python
import math

import jax
import jax.numpy as jnp
from jax import lax
from jax.sharding import PartitionSpec as P

HEADS = 12
DH = 64
FF = 3072
LEN = 1024


EPS = 1e-05
NEG = -1e30


def layer_norm(values, gain_vec, shift_vec):
    row_mean = jnp.mean(values, axis=-1, keepdims=True)
    centred = values - row_mean
    variance = jnp.mean(centred * centred, axis=-1, keepdims=True)
    return centred * lax.rsqrt(variance + EPS) * gain_vec + shift_vec


def gelu_exact(values):
    return jax.nn.gelu(values, approximate=False)


def contract_rows(first_op, second_op):
    return lax.dot_general(
        first_op, second_op, (((0,), (0,)), ((), ())), preferred_element_type=jnp.float32
    )


def contract_cols(first_op, second_op):
    return lax.dot_general(
        first_op, second_op, (((1,), (1,)), ((), ())), preferred_element_type=jnp.float32
    )


def row_pieces(qkv_b, seg_start, block_start, qblock):
    row_start = block_start // LEN * LEN
    query_rows = lax.dynamic_slice_in_dim(qkv_b, block_start, qblock, 0).reshape(
        qblock, 3, HEADS, DH
    )
    row_all = qkv_b.reshape(LEN, 3, HEADS, DH)
    seg_query = lax.dynamic_slice_in_dim(seg_start, block_start, qblock, 0)
    allowed = seg_query[:, None] == seg_start[None, :]
    score_scale = 1.0 / math.sqrt(DH)
    scores = (
        jnp.einsum(
            "qhd,khd->hqk", query_rows[:, 0], row_all[:, 1], preferred_element_type=jnp.float32
        )
        * score_scale
    )
    scores = jnp.where(allowed[None], scores, NEG)
    return (query_rows[:, 0], row_all[:, 1], row_all[:, 2], row_start, scores)


def shards(
    tokens,
    cotangent,
    seg_start,
    dispatch_slot,
    ln1_gain,
    ln1_shift,
    w_qkv,
    w_attn_out,
    ln2_gain,
    ln2_shift,
    w_in,
    w_out,
):
    tok_count = tokens.shape[0]
    feat_width = tokens.shape[1]
    n_expert = lax.axis_size("expert")
    group_size = n_expert // 2
    capacity = 2 * tok_count // n_expert
    n_slots = n_expert * capacity
    qblock = min(512, LEN)
    n_blocks = tok_count // qblock
    score_scale = 1.0 / math.sqrt(DH)
    own_expert = lax.axis_index("expert") // group_size
    inputs = tokens.astype(jnp.float32)
    normed_one, ln1_back = jax.vjp(layer_norm, inputs, ln1_gain, ln1_shift)
    normed_one_b = normed_one.astype(jnp.bfloat16)
    qkv_b = jnp.dot(normed_one_b, w_qkv, preferred_element_type=jnp.float32).astype(jnp.bfloat16)

    def forward_block(block_index):
        block_start = block_index * qblock
        queries, keys_row, values_row, row_start, scores = row_pieces(
            qkv_b, seg_start, block_start, qblock
        )
        top_score = jnp.max(scores, axis=-1, keepdims=True)
        shifted = jnp.exp(scores - top_score)
        totals = jnp.sum(shifted, axis=-1, keepdims=True)
        probs_b = (shifted / totals).astype(jnp.bfloat16)
        mixed_rows = jnp.einsum(
            "hqk,khd->qhd", probs_b, values_row, preferred_element_type=jnp.float32
        )
        return (
            mixed_rows.reshape(qblock, feat_width).astype(jnp.bfloat16),
            (top_score + jnp.log(totals))[..., 0],
        )

    mixed_blocks, lse_all = lax.map(forward_block, jnp.arange(n_blocks, dtype=jnp.int32))
    mixed_b = mixed_blocks.reshape(tok_count, feat_width)
    residual = inputs + jnp.dot(mixed_b, w_attn_out, preferred_element_type=jnp.float32)
    normed_two, ln2_back = jax.vjp(layer_norm, residual, ln2_gain, ln2_shift)
    normed_two_b = normed_two.astype(jnp.bfloat16)
    positions = jnp.arange(tok_count, dtype=jnp.int32)
    source_of = (
        jnp.full((n_slots,), tok_count, jnp.int32).at[dispatch_slot].set(positions, mode="drop")
    )
    zero_row = jnp.zeros((1, feat_width), jnp.bfloat16)
    send_rows = jnp.take(
        jnp.concatenate([normed_two_b, zero_row], axis=0), source_of, axis=0
    ).reshape(n_expert, capacity, feat_width)
    expert_in = lax.dynamic_index_in_dim(w_in, own_expert, 0, keepdims=False)
    expert_out = lax.dynamic_index_in_dim(w_out, own_expert, 0, keepdims=False)
    received = lax.all_to_all(send_rows, "expert", split_axis=0, concat_axis=0, tiled=True)
    flat_rows = received.reshape(-1, feat_width)
    hidden_pre = jnp.dot(flat_rows, expert_in, preferred_element_type=jnp.float32)
    hidden_b = gelu_exact(hidden_pre).astype(jnp.bfloat16)
    result = jnp.dot(hidden_b, expert_out, preferred_element_type=jnp.float32).astype(jnp.bfloat16)
    shape_lead = received.shape[:2]
    expert_rows_b, hidden_pre, received = (
        result.reshape(received.shape),
        hidden_pre.reshape(shape_lead + (FF,)),
        received,
    )
    returned = lax.all_to_all(expert_rows_b, "expert", split_axis=0, concat_axis=0, tiled=True)
    ffn_tok = jnp.take(
        jnp.concatenate([returned.reshape(n_slots, feat_width), zero_row], axis=0),
        dispatch_slot,
        axis=0,
    )
    result_out = (residual + ffn_tok.astype(jnp.float32)).astype(jnp.bfloat16)
    grad_out = cotangent.astype(jnp.float32)
    grad_send = jnp.take(jnp.concatenate([cotangent, zero_row], axis=0), source_of, axis=0).reshape(
        n_expert, capacity, feat_width
    )
    grad_expert = lax.all_to_all(grad_send, "expert", split_axis=0, concat_axis=0, tiled=True)
    grad_flat = grad_expert.reshape(n_slots, feat_width)
    rows_flat = received.reshape(n_slots, feat_width)
    pre_flat = hidden_pre.reshape(n_slots, FF)
    hidden_value, gelu_back = jax.vjp(gelu_exact, pre_flat)
    d_hidden = contract_cols(grad_flat, expert_out)
    d_pre_b = gelu_back(d_hidden)[0].astype(jnp.bfloat16)
    d_rows = contract_cols(d_pre_b, expert_in).astype(jnp.bfloat16)
    grad_back = lax.all_to_all(
        d_rows.reshape(n_expert, capacity, feat_width),
        "expert",
        split_axis=0,
        concat_axis=0,
        tiled=True,
    )
    d_normed_two = jnp.take(
        jnp.concatenate([grad_back.reshape(n_slots, feat_width), zero_row], axis=0),
        dispatch_slot,
        axis=0,
    ).astype(jnp.float32)
    part_in_t = contract_rows(d_pre_b, rows_flat)
    part_out = contract_rows(hidden_value.astype(jnp.bfloat16), grad_flat)
    which = (jnp.arange(2, dtype=jnp.int32) == own_expert)[:, None, None]
    padded_in = jnp.where(which, part_in_t[None], 0.0)
    padded_out = jnp.where(which, part_out[None], 0.0)
    group_in_t, group_out = (
        lax.psum_scatter(padded_in, "expert", scatter_dimension=1, tiled=True),
        lax.psum_scatter(padded_out, "expert", scatter_dimension=1, tiled=True),
    )
    summed_in_t, summed_out = (
        lax.psum(group_in_t.astype(jnp.bfloat16), "dp").astype(jnp.float32),
        lax.psum(group_out.astype(jnp.bfloat16), "dp").astype(jnp.float32),
    )
    d_resid_norm, grad_ln2_gain, grad_ln2_shift = ln2_back(d_normed_two)
    d_resid = grad_out + d_resid_norm
    d_branch_b = d_resid.astype(jnp.bfloat16)
    grad_w_attn_out = contract_rows(mixed_b, d_branch_b)
    d_mixed_b = contract_cols(d_branch_b, w_attn_out).astype(jnp.bfloat16)

    def backward_block(state_pair, inputs_block):
        key_grads, value_grads = state_pair
        block_index, lse_block = inputs_block
        block_start = block_index * qblock
        queries, keys_row, values_row, row_start, scores = row_pieces(
            qkv_b, seg_start, block_start, qblock
        )
        attn_probs = jnp.exp(scores - lse_block[:, :, None])
        grad_rows = lax.dynamic_slice_in_dim(d_mixed_b, block_start, qblock, 0).reshape(
            qblock, HEADS, DH
        )
        d_probs = jnp.einsum(
            "qhd,khd->hqk", grad_rows, values_row, preferred_element_type=jnp.float32
        )
        delta_rows = jnp.sum(attn_probs * d_probs, axis=-1, keepdims=True)
        d_scores = (attn_probs * (d_probs - delta_rows)).astype(jnp.bfloat16)
        d_query = (
            jnp.einsum("hqk,khd->qhd", d_scores, keys_row, preferred_element_type=jnp.float32)
            * score_scale
        )
        d_keys = (
            jnp.einsum("hqk,qhd->khd", d_scores, queries, preferred_element_type=jnp.float32)
            * score_scale
        )
        d_values = jnp.einsum(
            "hqk,qhd->khd",
            attn_probs.astype(jnp.bfloat16),
            grad_rows,
            preferred_element_type=jnp.float32,
        )
        old_keys = key_grads
        key_grads = old_keys + d_keys.reshape(LEN, feat_width)
        old_values = value_grads
        value_grads = old_values + d_values.reshape(LEN, feat_width)
        return ((key_grads, value_grads), d_query.reshape(qblock, feat_width))

    empty_grads = jnp.zeros((tok_count, feat_width), jnp.float32)
    (key_grads, value_grads), query_blocks = lax.scan(
        backward_block, (empty_grads, empty_grads), (jnp.arange(n_blocks, dtype=jnp.int32), lse_all)
    )
    query_grads = query_blocks.reshape(tok_count, feat_width)
    d_qkv = (
        jnp.stack([query_grads, key_grads, value_grads], axis=1)
        .reshape(tok_count, 3 * feat_width)
        .astype(jnp.bfloat16)
    )
    grad_w_qkv = contract_rows(normed_one_b, d_qkv)
    d_normed_one = contract_cols(d_qkv, w_qkv)
    d_inputs_norm, grad_ln1_gain, grad_ln1_shift = ln1_back(d_normed_one)
    grad_tokens = d_resid + d_inputs_norm
    modality = dispatch_slot // capacity // group_size
    local_counts = jnp.sum(
        (modality[:, None] == jnp.arange(2, dtype=jnp.int32)[None, :]).astype(jnp.float32), axis=0
    )
    reduced = lax.psum(
        (
            grad_w_qkv,
            grad_w_attn_out,
            grad_ln1_gain,
            grad_ln1_shift,
            grad_ln2_gain,
            grad_ln2_shift,
            local_counts,
        ),
        ("dp", "expert"),
    )
    all_counts = reduced[6]
    factor = jnp.sum(all_counts) / (2.0 * all_counts)
    grad_w_in = jnp.transpose(summed_in_t, (0, 2, 1)) * factor[:, None, None]
    grad_w_out = summed_out * factor[:, None, None]
    return (
        result_out,
        grad_tokens,
        reduced[2],
        reduced[3],
        reduced[0],
        reduced[1],
        reduced[4],
        reduced[5],
        grad_w_in,
        grad_w_out,
        all_counts.astype(jnp.int32),
    )


def solution(mesh):
    return jax.shard_map(
        shards,
        mesh=mesh,
        in_specs=(
            P(("dp", "expert"), None),
            P(("dp", "expert"), None),
            P(("dp", "expert")),
            P(("dp", "expert")),
            P(),
            P(),
            P(),
            P(),
            P(),
            P(),
            P(),
            P(),
        ),
        out_specs=(
            P(("dp", "expert"), None),
            P(("dp", "expert"), None),
            P(),
            P(),
            P(),
            P(),
            P(),
            P(),
            P(None, None, "expert"),
            P(None, "expert", None),
            P(),
        ),
        check_vma=False,
    )
```

profile of v0, /device:TPU:9, one launch (start us, length us, event | category | flops | bytes accessed | tf_op | source)
XLA Modules:
  0.0 1345.5 jit_solution(15896508103572154383)
XLA Ops:
  8.7 4.4 scatter_custom_fusion
  19.4 5.9 convolution_convert_fusion
  25.3 6.7 copy.44
  32.0 92.0 %while.27 = (s32[]{:T(128)}, bf16[2,512,768]{2,1,0:T(8,128)(2,1)}, f32[2,12,512]{2,1,0:T(8,128)}, s32[2]{0:T(128)S(1)}, s32[1024]{0:T(1024)S(1)}, /*index=5*/bf1...) while((s32[]{:T(128)}, bf16[2,512,768]{2,1,0:T(8,128)(2,1)}, ...), condition=%wide.region_5.6_spmd, body=%wide.region_2.5_spmd.sunk | while | flops 1687021568 | bytes 191465728 | solution.py:106
  35.5 12.1 fusion.114
  47.6 12.3 fusion.115
  59.9 3.1 copy-done.1
  63.0 9.9 fusion.116
  81.4 12.1 fusion.114
  93.5 12.3 fusion.115
  105.8 3.1 copy-done.1
  108.9 9.9 fusion.116
  124.0 3.8 fusion.77
  133.4 11.7 gather_fusion.2
  145.1 11.8 gather_fusion
  156.9 4.9 broadcast_select_fusion.2
  161.8 5.6 all-to-all-start
  168.0 67.5 %all-to-all-done = bf16[8,256,768]{2,1,0:T(8,128)(2,1)} async-done(((bf16[8,256,768]{2,1,0:T(8,128)(2,1)}), bf16[8,256,768]{2,1,0:T(8,128)(2,1)}, u32[]{:S(2)}, u32[]{:S(2)}) %all-to-all-start) | async-done | bytes 3145760 | tf_op jit(solution)/shard_map/all_to_all | solution.py:121
  235.4 8.0 all-to-all-start.2
  243.4 64.3 %multiply_convert_fusion.1 = (bf16[2048,3072]{1,0:T(8,128)(2,1)}, f32[2048,3072]{1,0:T(8,128)}, f32[2048,3072]{1,0:T(8,128)}) fusion(bf16[2048,768]{1,0:T(8,128)(2,1)} %bitcast.11, bf16[2,768,3072]{2,1,0:T(8,128)(2,1)} %param.30, s32[]{:T(128)S(6)} %select_n.60), kind=kOutput, calls=%fused_computation.47 | convolution fusion | flops 10072621056 | bytes 70778880 | tf_op jit(solution)/shard_map/dot_general | solution.py:123
  307.7 3.7 all-to-all-done.2
  311.4 33.4 %add_convert_fusion = bf16[2048,3072]{1,0:T(8,128)(2,1)} fusion(f32[2048,3072]{1,0:T(8,128)} %get-tuple-element.283, f32[2048,3072]{1,0:T(8,128)} %get-tuple-element.304, bf16[2048,768]{1,0:T(8,128)(2,1)} %bitcast.17, bf16[2,3072,768]{2,1,0:T(8,128)(2,1)} %param.31, s32[]{:T(128)S(6)} %select_n.60), kind=kOutput, calls=%fused_computation.46 | convolution fusion | flops 9751756800 | bytes 70778880 | tf_op jit(solution)/shard_map/dot_general | solution.py:36
  344.8 14.1 %fusion.79 = f32[3072,768]{1,0:T(8,128)S(1)} fusion(bf16[2048,3072]{1,0:T(8,128)(2,1)} %add_convert_fusion, bf16[2048,768]{1,0:T(8,128)(2,1)} %bitcast.11), kind=kOutput, calls=%fused_computation.163 | convolution fusion | flops 9663676416 | bytes 25165824 | tf_op jit(solution)/shard_map/dot_general | solution.py:30
  358.9 14.3 %fusion.80 = f32[3072,768]{1,0:T(8,128)S(1)} fusion(bf16[2048,3072]{1,0:T(8,128)(2,1)} %get-tuple-element.282, bf16[2048,768]{1,0:T(8,128)(2,1)} %bitcast.17), kind=kOutput, calls=%fused_computation.164 | convolution fusion | flops 9663676416 | bytes 25165824 | tf_op jit(solution)/shard_map/dot_general | solution.py:30
  373.2 13.1 broadcast_select_fusion
  387.1 15.5 %fusion.40 = bf16[2048,768]{1,0:T(8,128)(2,1)} fusion(bf16[2048,3072]{1,0:T(8,128)(2,1)} %add_convert_fusion, bf16[2,768,3072]{2,1,0:T(8,128)(2,1)} %param.30, s32[]{:T(128)S(6)} %select_n.60), kind=kOutput, calls=%fused_computation.92 | convolution fusion | flops 9665249280 | bytes 20447236 | tf_op jit(solution)/shard_map/dot_general | solution.py:36
  402.5 8.0 all-to-all-start.3
  410.5 15.4 %fusion.43 = bf16[2048,768]{1,0:T(8,128)(2,1)} fusion(bf16[2048,3072]{1,0:T(8,128)(2,1)} %get-tuple-element.282, bf16[2,3072,768]{2,1,0:T(8,128)(2,1)} %param.31, s32[]{:T(128)S(6)} %select_n.60), kind=kOutput, calls=%fused_computation.93 | convolution fusion | flops 9665249280 | bytes 20447236 | tf_op jit(solution)/shard_map/dot_general | solution.py:125
  426.0 106.8 %all-to-all-done.3 = bf16[8,256,768]{2,1,0:T(8,128)(2,1)} async-done(((bf16[8,256,768]{2,1,0:T(8,128)(2,1)}), bf16[8,256,768]{2,1,0:T(8,128)(2,1)}, u32[]{:S(2)}, u32[]{:S(2)}) %all-to-all-start.3) | async-done | bytes 3145760 | tf_op jit(solution)/shard_map/all_to_all | solution.py:151
  532.8 8.7 all-to-all-start.1
  542.1 3.8 concatenate.15
  545.9 99.7 %all-to-all-done.1 = bf16[8,256,768]{2,1,0:T(8,128)(2,1)} async-done(((bf16[8,256,768]{2,1,0:T(8,128)(2,1)}), bf16[8,256,768]{2,1,0:T(8,128)(2,1)}, u32[]{:S(2)}, u32[]{:S(2)}) %all-to-all-start.1) | async-done | bytes 3145760 | tf_op jit(solution)/shard_map/all_to_all | solution.py:132
  645.6 3.8 concatenate.13
  649.3 7.9 gather_fusion.3
  657.2 7.9 gather_fusion.1
  665.2 4.0 fusion.52
  669.3 4.6 fusion.74
  679.2 30.5 %reduce-scatter.5.cloned.1.call-done = f32[2,384,768]{2,1,0:T(8,128)} async-done(((f32[2,3072,768]{2,1,0:T(8,128)}), f32[2,384,768]{2,1,0:T(8,128)}) %reduce-scatter.5.cloned.1.call-update) | async-done | bytes 2359312 | tf_op jit(solution)/shard_map/reduce_scatter | solution.py:170
  712.6 184.7 %reduce-scatter.3.cloned.1.call-done = f32[2,384,768]{2,1,0:T(8,128)} async-done(((f32[2,3072,768]{2,1,0:T(8,128)}), f32[2,384,768]{2,1,0:T(8,128)}) %reduce-scatter.3.cloned.1.call-update) | async-done | bytes 2359312 | tf_op jit(solution)/shard_map/reduce_scatter | solution.py:169
  900.2 208.6 %while.28 = (s32[]{:T(128)}, f32[1024,768]{0,1:T(8,128)}, f32[1024,768]{0,1:T(8,128)}, bf16[2,512,768]{2,1,0:T(8,128)(2,1)}, s32[2]{0:T(128)S(1)}, /*index=5*/bf...) while((s32[]{:T(128)}, f32[1024,768]{0,1:T(8,128)}, ...), condition=%wide.region_13.16_spmd.clone, body=%wide.region_11.15_spmd.clone.sunk | while | flops 4126140416 | bytes 332425696 | solution.py:219
  912.3 10.3 fusion.122
  922.7 13.5 %fusion.123 = f32[12,64,1024]{2,1,0:T(8,128)} fusion(bf16[512,12,64]{0,2,1:T(8,128)(2,1)S(1)} %bitcast.171, f32[12,512,1024]{2,1,0:T(8,128)} %fusion.122, f32[12,512]{1,0:T(8,128)S(1)} %copy-done.21, pred[512,1024]{1,0:T(8,128)(4,1)S(1)} %copy-done.4), kind=kOutput, calls=%fused_computation.26.clone.1 | convolution fusion | flops 830472192 | bytes 29646848 | tf_op jit(solution)/shard_map/while/body/eval_jaxpr/hqk,qhd->khd/dot_general | solution.py:206
  936.2 18.8 %multiply_reduce_fusion.3 = (f32[12,512]{1,0:T(8,128)}, f32[12,512,1024]{2,1,0:T(8,128)}) fusion(f32[12,512,1024]{2,1,0:T(8,128)} %fusion.122, f32[12,512]{1,0:T(8,128)} %dynamic-slice_bitcast_fusion.2, pred[512,1024]{1,0:T(8,128)(4,1)} %broadcast_compare_fusion.5, bf16[512,12,64]{0,2,1:T(8,128)(2,1)} %bitcast.170, ...), kind=kOutput, calls=%fused_computation.23.clone.1 | convolution fusion | flops 836757504 | bytes 53272576 | tf_op jit(solution)/shard_map/while/body/eval_jaxpr/qhd,khd->hqk/dot_general | solution.py:193
  955.0 23.2 %multiply_convert_fusion.3 = bf16[12,512,1024]{2,1,0:T(8,128)(2,1)} fusion(f32[12,512,1024]{2,1,0:T(8,128)} %get-tuple-element.406, f32[12,512,1024]{2,1,0:T(8,128)} %fusion.122, f32[12,512]{1,0:T(8,128)} %get-tuple-element.407, f32[12,512]{1,0:T(8,128)} %dynamic-slice_bitcast_fusion.2, pred[512,1024]{1,0:T(8,128)(4,1)} %broadcast_compare_fusion.5), kind=kLoop, calls=%fused_computation.22.clone.1 | loop fusion | flops 37748736 | bytes 63488000 | tf_op jit(solution)/shard_map/while/body/eval_jaxpr/convert_element_type | solution.py:197
  978.2 9.8 convolution_multiply_fusion.5
  988.0 7.3 convolution_multiply_fusion.4
  1017.2 10.1 fusion.122
  1027.3 13.1 fusion.123
  1040.4 18.8 %multiply_reduce_fusion.3 = (f32[12,512]{1,0:T(8,128)}, f32[12,512,1024]{2,1,0:T(8,128)}) fusion(f32[12,512,1024]{2,1,0:T(8,128)} %fusion.122, f32[12,512]{1,0:T(8,128)} %dynamic-slice_bitcast_fusion.2, pred[512,1024]{1,0:T(8,128)(4,1)} %broadcast_compare_fusion.5, bf16[512,12,64]{0,2,1:T(8,128)(2,1)} %bitcast.170, ...), kind=kOutput, calls=%fused_computation.23.clone.1 | convolution fusion | flops 836757504 | bytes 53272576 | tf_op jit(solution)/shard_map/while/body/eval_jaxpr/qhd,khd->hqk/dot_general | solution.py:193
  1059.2 22.2 %multiply_convert_fusion.3 = bf16[12,512,1024]{2,1,0:T(8,128)(2,1)} fusion(f32[12,512,1024]{2,1,0:T(8,128)} %get-tuple-element.406, f32[12,512,1024]{2,1,0:T(8,128)} %fusion.122, f32[12,512]{1,0:T(8,128)} %get-tuple-element.407, f32[12,512]{1,0:T(8,128)} %dynamic-slice_bitcast_fusion.2, pred[512,1024]{1,0:T(8,128)(4,1)} %broadcast_compare_fusion.5), kind=kLoop, calls=%fused_computation.22.clone.1 | loop fusion | flops 37748736 | bytes 63488000 | tf_op jit(solution)/shard_map/while/body/eval_jaxpr/convert_element_type | solution.py:197
  1081.4 9.8 convolution_multiply_fusion.5
  1091.2 7.3 convolution_multiply_fusion.4
  1108.9 3.0 copy.49
  1115.0 5.0 pad_maximum_fusion
  1120.0 6.6 copy.51
  1126.7 4.9 fusion.78
  1131.6 6.7 fusion.69
  1139.6 8.1 fusion.73
  1150.1 43.9 %all-reduce.4 = (f32[768]{0:T(1024)}, f32[768]{0:T(1024)}, f32[768]{0:T(1024)}, f32[768]{0:T(1024)}, f32[2]{0:T(128)}) all-reduce(f32[768]{0:T(1024)} %get-tuple-element.234, f32[768]{0:T(1024)} %get-tuple-element.238, f32[768]{0:T(1024)} %get-tuple-element.236, ...), channel_id=1, replica_groups=mesh['dp'=4,'expert'=8] {'dp','expert'}, use_global_device_ids=true, to_apply=%region_17.20 | all-reduce | flops 3074 | bytes 24592 | tf_op jit(solution)/shard_map/psum | solution.py:236
  1197.9 6.1 add_add_fusion.2
  1204.0 4.4 convert_multiply_fusion.2
  1208.4 3.1 copy.52
  1211.4 119.4 %all-reduce.10.cloned.1.call-done = (f32[768,2304]{1,0:T(8,128)}, f32[768,768]{1,0:T(8,128)}) async-done(((f32[768,2304]{1,0:T(8,128)}, f32[768,768]{1,0:T(8,128)}), (f32[768,2304]{1,0:T(8,128)}, f32[768,768]{1,0:T(8,128)})) %all-reduce.10.cloned.1.call-update) | async-done | bytes 9437200 | tf_op jit(solution)/shard_map/psum | solution.py:236
  1330.8 6.6 copy.110
  (222 shorter events, 96.4 us)
Async XLA Ops:
  7.2 12.2 copy-start
  7.2 12.2 copy-start.47
  13.1 6.2 copy-start.57
  14.3 5.0 copy-start.14
  16.1 2.6 copy-start.32
  25.3 6.7 copy-start.25
  47.6 15.4 %copy-start.1 = (f32[12,512,1024]{2,1,0:T(8,128)S(1)}, f32[12,512,1024]{2,1,0:T(8,128)}, u32[]{:S(2)}) copy-start(f32[12,512,1024]{2,1,0:T(8,128)} %get-tuple-element.395) | copy-start | bytes 75497472 | tf_op jit(solution)/shard_map/while
  63.0 9.9 copy-start.27
  93.5 15.4 %copy-start.1 = (f32[12,512,1024]{2,1,0:T(8,128)S(1)}, f32[12,512,1024]{2,1,0:T(8,128)}, u32[]{:S(2)}) copy-start(f32[12,512,1024]{2,1,0:T(8,128)} %get-tuple-element.395) | copy-start | bytes 75497472 | tf_op jit(solution)/shard_map/while
  108.9 9.9 copy-start.27
  127.8 3.8 copy-start.11
  127.8 2.6 copy-start.17
  127.8 3.8 copy-start.29
  127.8 3.8 copy-start.42
  127.8 3.8 copy-start.54
  130.3 1.8 copy-start.34
  145.1 11.8 copy-start.53
  161.8 73.6 %all-to-all-start = ((bf16[8,256,768]{2,1,0:T(8,128)(2,1)}), bf16[8,256,768]{2,1,0:T(8,128)(2,1)}, u32[]{:S(2)}, u32[]{:S(2)}) async-start(bf16[8,256,768]{2,1,0:T(8,128)(2,1)} %bitcast.175), calls=%async_computation | async-start | bytes 6291456 | tf_op jit(solution)/shard_map/all_to_all | solution.py:121
  235.4 76.0 %all-to-all-start.2 = ((bf16[8,256,768]{2,1,0:T(8,128)(2,1)}), bf16[8,256,768]{2,1,0:T(8,128)(2,1)}, u32[]{:S(2)}, u32[]{:S(2)}) async-start(bf16[8,256,768]{2,1,0:T(8,128)(2,1)} %bitcast.174), calls=%async_computation.2 | async-start | bytes 6291456 | tf_op jit(solution)/shard_map/all_to_all | solution.py:143
  243.4 466.4 %reduce-scatter.5.cloned.1.call-start = ((), (), s32[]{:S(2)}) async-start(), calls=%async_computation.7 | async-start | bytes 21233664 | tf_op jit(solution)/shard_map/reduce_scatter | solution.py:170
  358.9 14.3 %copy-start.55 = (pred[2]{0:T(512)(128)(4,1)S(1)}, pred[2]{0:T(512)(128)(4,1)}, u32[]{:S(2)}) copy-start(pred[2]{0:T(512)(128)(4,1)} %iota_compare_fusion) | copy-start | bytes 10
  386.3 511.0 %reduce-scatter.3.cloned.1.call-start = ((), (), s32[]{:S(2)}) async-start(), calls=%async_computation.6 | async-start | bytes 21233664 | tf_op jit(solution)/shard_map/reduce_scatter | solution.py:169
  402.5 130.3 %all-to-all-start.3 = ((bf16[8,256,768]{2,1,0:T(8,128)(2,1)}), bf16[8,256,768]{2,1,0:T(8,128)(2,1)}, u32[]{:S(2)}, u32[]{:S(2)}) async-start(bf16[8,256,768]{2,1,0:T(8,128)(2,1)} %bitcast.181), calls=%async_computation.3 | async-start | bytes 6291456 | tf_op jit(solution)/shard_map/all_to_all | solution.py:151
  532.8 8.7 copy-start.50
  532.8 112.7 %all-to-all-start.1 = ((bf16[8,256,768]{2,1,0:T(8,128)(2,1)}), bf16[8,256,768]{2,1,0:T(8,128)(2,1)}, u32[]{:S(2)}, u32[]{:S(2)}) async-start(bf16[8,256,768]{2,1,0:T(8,128)(2,1)} %bitcast.180), calls=%async_computation.1 | async-start | bytes 6291456 | tf_op jit(solution)/shard_map/all_to_all | solution.py:132
  541.5 662.4 %all-reduce.12.cloned.1.call-start = ((), (), s32[]{:S(2)}) async-start(), calls=%async_computation.9 | async-start | bytes 4718592 | tf_op jit(solution)/shard_map/psum | solution.py:173
  645.6 3.8 copy-start.46
  657.2 7.9 copy-start.30
  657.2 7.9 copy-start.35
  657.2 7.9 copy-start.43
  665.1 4.1 copy-start.41
  665.1 4.1 copy-start.12
  665.1 4.1 copy-start.19
  665.2 4.1 copy-start.52
  669.3 4.6 copy-start.18
  673.9 2.8 copy-start.56
  712.6 187.7 %copy-start.26 = (s32[1024]{0:T(1024)S(1)}, s32[1024]{0:T(1024)}, u32[]{:S(2)}) copy-start(s32[1024]{0:T(1024)} %param.22) | copy-start | bytes 12292
  900.2 430.6 %all-reduce.10.cloned.1.call-start = ((), (), s32[]{:S(2)}) async-start(), calls=%async_computation.8 | async-start | bytes 18874368 | tf_op jit(solution)/shard_map/psum | solution.py:236
  909.0 3.4 copy-start.2
  912.3 10.3 copy-start.4
  912.3 10.3 copy-start.10
  912.3 10.3 copy-start.21
  988.0 7.3 copy-start.5
  988.0 7.3 copy-start.7
  988.0 7.6 copy-start.9
  1013.8 3.4 copy-start.2
  1017.2 10.1 copy-start.4
  1017.2 10.1 copy-start.10
  1017.2 10.1 copy-start.21
  1091.2 7.3 copy-start.5
  1091.2 7.3 copy-start.7
  1091.2 7.6 copy-start.9
  1126.7 4.9 copy-start.15
  1126.7 4.9 copy-start.22
  1126.7 4.9 copy-start.33
  1126.7 4.9 copy-start.37
  1126.7 4.9 copy-start.48
  1126.7 4.9 copy-start.58
  1139.6 8.1 copy-start.39
  1139.6 8.1 copy-start.16
  1139.6 8.1 copy-start.49
  1147.7 2.3 copy-start.20
  1147.7 50.1 %copy-start.45 = (f32[1024]{0:T(1024)S(1)}, f32[1024]{0:T(1024)}, u32[]{:S(2)}) copy-start(f32[1024]{0:T(1024)} %copy-done.44) | copy-start | bytes 12292
  1330.8 6.6 copy-start.23
  (16 other events, 19.5 us)
Sparse Core Ops, SparseCore 0:
  386.4 323.2 reduce-scatter.4
  712.1 185.1 reduce-scatter.2
  900.4 74.0 all-reduce.11
  1138.4 192.3 all-reduce.9
where the time goes:
time: 1360 us; the launch traced here: 1350 us
  waiting for transfers between devices  613 us (45%)
  matrix products  352 us (26%)
  local copies, waits for them, and re-layouts  147 us (11%)
  other arithmetic  141 us (10%)
  blocking collectives  43.9 us (3%)
  starting transfers between devices  30.5 us (2%)
  between operations  14.4 us (1%)
    reduce_scatter x1, waiting for transfers between devices, shards(): lax.psum_scatter(padded_in, 'expert', scatter_dimension=1, tiled=True)  185 us
    psum x1, waiting for transfers between devices, shards(): lax.psum((grad_w_qkv, grad_w_attn_out, grad_ln1_gain, grad_ln1_shift, gra...  119 us
    all_to_all x1, waiting for transfers between devices, shards(): lax.all_to_all(d_rows.reshape(n_expert, capacity, feat_width), 'expert',...  107 us
    all_to_all x1, waiting for transfers between devices, shards(): lax.all_to_all(expert_rows_b, 'expert', split_axis=0, concat_axis=0, tile...  99.7 us
    all_to_all x1, waiting for transfers between devices, shards(): lax.all_to_all(send_rows, 'expert', split_axis=0, concat_axis=0, tiled=True)  67.5 us
    dot_general x1, matrix products, shards(): jnp.dot(flat_rows, expert_in, preferred_element_type=jnp.float32)  64.3 us
    dot_general x4, matrix products, contract_cols(): lax.dot_general(first_op, second_op, (((1,), (1,)), ((), ())), preferred_...  59.6 us
    convert_element_type x2, other arithmetic, backward_block(): d_scores = (attn_probs * (d_probs - delta_rows)).astype(jnp.bfloat16)  45.4 us
  transfers between devices with their start and end apart: 8, of which 7 were waited for; matrix products, arithmetic and copies ran while one was open for 29% of the time, Pallas kernels for 0%

commit v1 on v0

v1 whole, which is shorter than its diff:
```python
import functools
import math

import jax
import jax.numpy as jnp
from jax import lax
from jax.experimental import pallas as pl
from jax.experimental.pallas import tpu as pltpu
from jax.sharding import PartitionSpec as P

HEADS = 12
DH = 64
LEN = 1024
NEG = -1e30
EPS = 1e-05
PAIR = 128
LOG2E = math.log2(math.e)
bf16 = jnp.bfloat16
f32 = jnp.float32
VMEM_BYTES = 56 << 20


def dot_nn(a, b):
    return lax.dot_general(a, b, (((1,), (0,)), ((), ())), preferred_element_type=f32)


def dot_nt(a, b):
    return lax.dot_general(a, b, (((1,), (1,)), ((), ())), preferred_element_type=f32)


def dot_tn(a, b):
    return lax.dot_general(a, b, (((0,), (0,)), ((), ())), preferred_element_type=f32)


def block_meta(seg, qb, win):
    nq=LEN//qb
    rows=seg.reshape(nq,qb)
    lo_s=jnp.min(rows,axis=1)[:,None]; hi_s=jnp.max(rows,axis=1)[:,None]
    pos=jnp.arange(LEN,dtype=jnp.int32)[None]
    hit=(seg[None]>=lo_s)&(seg[None]<=hi_s)
    first=jnp.min(jnp.where(hit,pos,LEN),axis=1)
    last=jnp.max(jnp.where(hit,pos+1,0),axis=1)
    lo=jnp.minimum(first//128*128, LEN-win)
    count=(last-lo+win-1)//win
    single=jnp.broadcast_to((jnp.max(count)==1).astype(jnp.int32),count.shape)
    return jnp.stack([lo,count,single])

def window(lo_ref, i, t, win, seg_col_ref):
    base=lo_ref[0,i]+t*win
    start=pl.multiple_of(jnp.minimum(base,LEN-win),128)
    seg_k=seg_col_ref[pl.ds(start,win),:]
    pos=start+lax.broadcasted_iota(jnp.int32,(win,PAIR),0)
    return start, jnp.where(pos>=base,seg_k,-1)

def fwd_kernel(qb, win, lo_ref, q_ref, k_ref, v_ref, seg_col_ref, seg_row_ref, o_ref, lse_ref, vt_ref):
    vt_ref[...]=v_ref[...].T
    c=LOG2E/math.sqrt(DH)
    def block(i,_,fast=False):
        r0=i*qb if fast else pl.multiple_of(i*qb,qb)
        q=q_ref[pl.ds(r0,qb),:]
        low=lax.broadcasted_iota(jnp.int32,(qb,PAIR),1)<DH
        zero=jnp.zeros_like(q)
        qs=(jnp.where(low,q,zero),jnp.where(low,zero,q))
        seg_q=seg_row_ref[:,pl.ds(r0,qb)]
        def one():
            start,seg_k=window(lo_ref,i,0,win,seg_col_ref)
            ok=jnp.concatenate([seg_k]*(qb//PAIR),axis=1)==seg_q
            kw=k_ref[pl.ds(start,win),:]
            res=[]
            for h in range(2):
                s=jnp.where(ok,dot_nt(kw,qs[h])*c,NEG)
                m=jnp.max(s,axis=0,keepdims=True)
                p=jnp.exp2(s-m)
                l=jnp.sum(p,axis=0,keepdims=True)
                vtw=vt_ref[h*DH:(h+1)*DH,pl.ds(start,win)]
                res.append((m,l,dot_nn(vtw,p.astype(bf16))))
            return res
        def win_step(t,carry):
            start,seg_k=window(lo_ref,i,t,win,seg_col_ref)
            ok=jnp.concatenate([seg_k]*(qb//PAIR),axis=1)==seg_q
            kw=k_ref[pl.ds(start,win),:]
            out=[]
            for h in range(2):
                m,l,acc=carry[h]
                s=jnp.where(ok,dot_nt(kw,qs[h])*c,NEG)
                mn=jnp.maximum(m,jnp.max(s,axis=0,keepdims=True))
                al=jnp.exp2(m-mn)
                p=jnp.exp2(s-mn)
                l=l*al+jnp.sum(p,axis=0,keepdims=True)
                vtw=vt_ref[h*DH:(h+1)*DH,pl.ds(start,win)]
                acc=acc*al+dot_nn(vtw,p.astype(bf16))
                out.append((mn,l,acc))
            return tuple(out)
        init=(jnp.full((1,qb),NEG,f32),jnp.zeros((1,qb),f32),jnp.zeros((DH,qb),f32))
        res=one() if fast else lax.fori_loop(0,lo_ref[1,i],win_step,(init,init))
        ot=jnp.concatenate([a/l for m,l,a in res],axis=0)
        o_ref[pl.ds(r0,qb),:]=ot.T.astype(bf16)
        lse_ref[0,:,pl.ds(r0,qb)]=jnp.concatenate([m+jnp.log2(l) for m,l,a in res],axis=0)
        return 0
    single=lo_ref[2,0]==1
    @pl.when(single)
    def _():
        low=lax.broadcasted_iota(jnp.int32,(qb,PAIR),1)<DH
        def scores(i,h):
            q=q_ref[i*qb:(i+1)*qb,:]
            zero=jnp.zeros_like(q)
            qh=jnp.where(low,q,zero) if h==0 else jnp.where(low,zero,q)
            start=pl.multiple_of(lo_ref[0,i],128)
            ok=jnp.concatenate([seg_col_ref[pl.ds(start,win),:]]*(qb//PAIR),axis=1)==seg_row_ref[:,i*qb:(i+1)*qb]
            return jnp.where(ok,dot_nt(k_ref[pl.ds(start,win),:],qh)*c,NEG)
        units=[(i,h) for i in range(LEN//qb) for h in range(2)]
        ahead=3
        queue=[scores(*u) for u in units[:ahead]]
        done={}
        for n,(i,h) in enumerate(units):
            s=queue.pop(0)
            m=jnp.max(s,axis=0,keepdims=True)
            if n+ahead<len(units): queue.append(scores(*units[n+ahead]))
            p=jnp.exp2(s-m)
            l=jnp.sum(p,axis=0,keepdims=True)
            start=pl.multiple_of(lo_ref[0,i],128)
            acc=dot_nn(vt_ref[h*DH:(h+1)*DH,pl.ds(start,win)],p.astype(bf16))
            done[h]=(acc/l,m+jnp.log2(l))
            if h==1:
                o_ref[i*qb:(i+1)*qb,:]=jnp.concatenate([done[0][0],done[1][0]],axis=0).T.astype(bf16)
                lse_ref[0,:,i*qb:(i+1)*qb]=jnp.concatenate([done[0][1],done[1][1]],axis=0)
    @pl.when(jnp.logical_not(single))
    def _():
        lax.fori_loop(0,LEN//qb,block,0)

def attn_fwd(qkv, meta, seg_col, seg_row, qb=256, win=512):
    nh=HEADS//2
    return pl.pallas_call(
        functools.partial(fwd_kernel,qb,win),
        out_shape=(jax.ShapeDtypeStruct((LEN,HEADS*DH),bf16),jax.ShapeDtypeStruct((nh,2,LEN),f32)),
        grid_spec=pltpu.PrefetchScalarGridSpec(num_scalar_prefetch=1,grid=(nh,),
            in_specs=[pl.BlockSpec((LEN,PAIR),lambda h,*_:(0,h)),
                      pl.BlockSpec((LEN,PAIR),lambda h,*_:(0,nh+h)),
                      pl.BlockSpec((LEN,PAIR),lambda h,*_:(0,2*nh+h)),
                      pl.BlockSpec((LEN,PAIR),lambda h,*_:(0,0)),
                      pl.BlockSpec((1,LEN),lambda h,*_:(0,0))],
            out_specs=[pl.BlockSpec((LEN,PAIR),lambda h,*_:(0,h)),
                       pl.BlockSpec((1,2,LEN),lambda h,*_:(h,0,0))],
            scratch_shapes=[pltpu.VMEM((PAIR,LEN),bf16)]),
        compiler_params=pltpu.CompilerParams(vmem_limit_bytes=VMEM_BYTES),
        name="attn_fwd",
    )(meta,qkv,qkv,qkv,seg_col,seg_row)

def bwd_kernel(qb, win, lo_ref, q_ref, k_ref, v_ref, dm_ref, o_ref, lse_ref, seg_col_ref, seg_row_ref, dq_ref, dk_ref, dv_ref, kt_ref, dka, dva):
    kt_ref[...]=k_ref[...].T
    dka[...]=jnp.zeros_like(dka); dva[...]=jnp.zeros_like(dva)
    c=LOG2E/math.sqrt(DH); scale=1.0/math.sqrt(DH)
    def block(i,_,fast=False):
        r0=i*qb if fast else pl.multiple_of(i*qb,qb)
        q=q_ref[pl.ds(r0,qb),:]; dm=dm_ref[pl.ds(r0,qb),:]
        low=lax.broadcasted_iota(jnp.int32,(qb,PAIR),1)<DH
        zero=jnp.zeros_like(q)
        qs=(jnp.where(low,q,zero),jnp.where(low,zero,q))
        dms=(jnp.where(low,dm,zero),jnp.where(low,zero,dm))
        seg_q=seg_row_ref[:,pl.ds(r0,qb)]
        prod=(dm.astype(f32)*o_ref[pl.ds(r0,qb),:].astype(f32)).T
        delta=[jnp.sum(prod[h*DH:(h+1)*DH],axis=0,keepdims=True) for h in range(2)]
        lse=[lse_ref[0,h:h+1,pl.ds(r0,qb)] for h in range(2)]
        def win_step(t,carry):
            start,seg_k=window(lo_ref,i,t,win,seg_col_ref)
            ok=jnp.concatenate([seg_k]*(qb//PAIR),axis=1)==seg_q
            kw=k_ref[pl.ds(start,win),:]; vw=v_ref[pl.ds(start,win),:]
            out=[]
            dk=dka[pl.ds(start,win),:]; dv=dva[pl.ds(start,win),:]
            for h in range(2):
                s=dot_nt(kw,qs[h])
                p=jnp.where(ok,jnp.exp2(s*c-lse[h]),0.0)
                dp=dot_nt(vw,dms[h])
                ds=(p*(dp-delta[h])).astype(bf16)
                dv=dv+dot_nn(p.astype(bf16),dms[h])
                dk=dk+dot_nn(ds,qs[h])
                out.append(carry[h]+dot_nn(kt_ref[h*DH:(h+1)*DH,pl.ds(start,win)],ds))
            dka[pl.ds(start,win),:]=dk; dva[pl.ds(start,win),:]=dv
            return tuple(out)
        init=jnp.zeros((DH,qb),f32)
        res=win_step(0,(init,init)) if fast else lax.fori_loop(0,lo_ref[1,i],win_step,(init,init))
        dq_ref[pl.ds(r0,qb),:]=(jnp.concatenate(res,axis=0)*scale).T.astype(bf16)
        return 0
    single=lo_ref[2,0]==1
    @pl.when(single)
    def _():
        low=lax.broadcasted_iota(jnp.int32,(qb,PAIR),1)<DH
        def half(x,h):
            zero=jnp.zeros_like(x)
            return jnp.where(low,x,zero) if h==0 else jnp.where(low,zero,x)
        def products(i,h):
            start=pl.multiple_of(lo_ref[0,i],128)
            qh=half(q_ref[i*qb:(i+1)*qb,:],h); dmh=half(dm_ref[i*qb:(i+1)*qb,:],h)
            return dot_nt(k_ref[pl.ds(start,win),:],qh),dot_nt(v_ref[pl.ds(start,win),:],dmh),qh,dmh
        units=[(i,h) for i in range(LEN//qb) for h in range(2)]
        ahead=2
        queue=[products(*u) for u in units[:ahead]]
        dqs={}
        for n,(i,h) in enumerate(units):
            s,dp,qh,dmh=queue.pop(0)
            if n+ahead<len(units): queue.append(products(*units[n+ahead]))
            start=pl.multiple_of(lo_ref[0,i],128)
            rows=slice(i*qb,(i+1)*qb)
            if h==0:
                prod=(dm_ref[rows,:].astype(f32)*o_ref[rows,:].astype(f32)).T
                ok=jnp.concatenate([seg_col_ref[pl.ds(start,win),:]]*(qb//PAIR),axis=1)==seg_row_ref[:,rows]
            delta=jnp.sum(prod[h*DH:(h+1)*DH],axis=0,keepdims=True)
            p=jnp.where(ok,jnp.exp2(s*c-lse_ref[0,h:h+1,rows]),0.0)
            ds=(p*(dp-delta)).astype(bf16)
            dva[pl.ds(start,win),:]+=dot_nn(p.astype(bf16),dmh)
            dka[pl.ds(start,win),:]+=dot_nn(ds,qh)
            dqs[h]=dot_nn(kt_ref[h*DH:(h+1)*DH,pl.ds(start,win)],ds)
            if h==1:
                dq_ref[rows,:]=(jnp.concatenate([dqs[0],dqs[1]],axis=0)*scale).T.astype(bf16)
    @pl.when(jnp.logical_not(single))
    def _():
        lax.fori_loop(0,LEN//qb,block,0)
    dk_ref[...]=(dka[...]*scale).astype(bf16)
    dv_ref[...]=dva[...].astype(bf16)

def attn_bwd(qkv, dmixed, mixed, lse, meta, seg_col, seg_row, qb=256, win=512, h0=0, nh=6):
    np_=HEADS//2
    col=lambda off: pl.BlockSpec((LEN,PAIR),lambda h,*_:(0,off+h0+h))
    out=pl.BlockSpec((LEN,PAIR),lambda h,*_:(0,h))
    sh=jax.ShapeDtypeStruct((LEN,nh*PAIR),bf16)
    return pl.pallas_call(
        functools.partial(bwd_kernel,qb,win),
        out_shape=(sh,sh,sh),
        grid_spec=pltpu.PrefetchScalarGridSpec(num_scalar_prefetch=1,grid=(nh,),
            in_specs=[col(0),col(np_),col(2*np_),col(0),col(0),
                      pl.BlockSpec((1,2,LEN),lambda h,*_:(h0+h,0,0)),
                      pl.BlockSpec((LEN,PAIR),lambda h,*_:(0,0)),
                      pl.BlockSpec((1,LEN),lambda h,*_:(0,0))],
            out_specs=[out,out,out],
            scratch_shapes=[pltpu.VMEM((PAIR,LEN),bf16),pltpu.VMEM((LEN,PAIR),f32),pltpu.VMEM((LEN,PAIR),f32)]),
        compiler_params=pltpu.CompilerParams(vmem_limit_bytes=VMEM_BYTES),
        name="attn_bwd",
    )(meta,qkv,qkv,qkv,dmixed,mixed,lse,seg_col,seg_row)

ROWS = 256


def full(*shape):
    return pl.BlockSpec(shape, lambda *_: (0,) * len(shape))


def rows_of(width):
    return pl.BlockSpec((ROWS, width), lambda i, *_: (i, 0))


def normalise(x):
    centred = x - jnp.mean(x, axis=-1, keepdims=True)
    rstd = lax.rsqrt(jnp.mean(centred * centred, axis=-1, keepdims=True) + EPS)
    return centred * rstd, rstd


def norm_back(u, gain, n, rstd):
    ug = u * gain
    return rstd * (
        ug - jnp.mean(ug, axis=-1, keepdims=True) - n * jnp.mean(ug * n, axis=-1, keepdims=True)
    )


def params():
    return pltpu.CompilerParams(vmem_limit_bytes=VMEM_BYTES)


def qkv_kernel(x_ref, gain_ref, shift_ref, w_ref, h1_ref, qkv_ref):
    n, _ = normalise(x_ref[...].astype(f32))
    h1 = (n * gain_ref[...] + shift_ref[...]).astype(bf16)
    h1_ref[...] = h1
    qkv_ref[...] = dot_nn(h1, w_ref[...]).astype(bf16)


def ln_qkv(tokens, gain, shift, w_qkv):
    t, d = tokens.shape
    return pl.pallas_call(
        qkv_kernel,
        grid=(t // ROWS,),
        in_specs=[rows_of(d), full(1, d), full(1, d), full(d, 3 * d)],
        out_specs=[rows_of(d), rows_of(3 * d)],
        out_shape=(
            jax.ShapeDtypeStruct((t, d), bf16),
            jax.ShapeDtypeStruct((t, 3 * d), bf16),
        ),
        compiler_params=params(),
        name="ln_qkv",
    )(tokens, gain, shift, w_qkv)


def proj_kernel(n_slots, x_ref, mixed_ref, cot_ref, slot_ref, w_ref, gain_ref, shift_ref,
                resid_ref, h2_ref, cotm_ref):
    resid = x_ref[...].astype(f32) + dot_nn(mixed_ref[...], w_ref[...])
    resid_ref[...] = resid
    n, _ = normalise(resid)
    h2_ref[...] = (n * gain_ref[...] + shift_ref[...]).astype(bf16)
    routed = slot_ref[...] < n_slots
    cotm_ref[...] = jnp.where(routed, cot_ref[...].astype(f32), 0.0).astype(bf16)


def proj_ln(tokens, mixed, cotangent, slot_col, w_attn_out, gain, shift, n_slots):
    t, d = tokens.shape
    return pl.pallas_call(
        functools.partial(proj_kernel, n_slots),
        grid=(t // ROWS,),
        in_specs=[rows_of(d), rows_of(d), rows_of(d), rows_of(1), full(d, d), full(1, d), full(1, d)],
        out_specs=[rows_of(d), rows_of(d), rows_of(d)],
        out_shape=(
            jax.ShapeDtypeStruct((t, d), f32),
            jax.ShapeDtypeStruct((t, d), bf16),
            jax.ShapeDtypeStruct((t, d), bf16),
        ),
        compiler_params=params(),
        name="proj_ln",
    )(tokens, mixed, cotangent, slot_col, w_attn_out, gain, shift)


def gelu_parts(v):
    half = 0.5 * (1.0 + lax.erf(v * math.sqrt(0.5)))
    bell = jnp.exp(-0.5 * v * v) * (1.0 / math.sqrt(2.0 * math.pi))
    return v * half, half + v * bell


def ffn_kernel(which_ref, h2_ref, cot_ref, win_ref, wout_ref, ffn_ref, dh2_ref, gin_ref, gout_ref):
    h2 = h2_ref[...]
    cot = cot_ref[...]
    win = win_ref[0]
    wout = wout_ref[0]
    pre = dot_nn(h2, win)
    d_hidden = dot_nt(cot, wout)
    hidden, slope = gelu_parts(pre)
    hidden = hidden.astype(bf16)
    d_pre = (d_hidden * slope).astype(bf16)
    gout_ref[...] = dot_tn(hidden, cot).astype(gout_ref.dtype)
    gin_ref[...] = dot_tn(d_pre, h2).astype(gin_ref.dtype)
    ffn = dot_nn(hidden, wout)
    dh2 = dot_nt(d_pre, win)

    @pl.when(pl.program_id(0) == 0)
    def _():
        ffn_ref[...] = ffn
        dh2_ref[...] = dh2

    @pl.when(pl.program_id(0) > 0)
    def _():
        ffn_ref[...] += ffn
        dh2_ref[...] += dh2


def ffn_both(which, h2, cot, w_in, w_out, chunk):
    t, d = h2.shape
    ff = w_in.shape[2]
    piece = pl.BlockSpec((chunk, d), lambda i, *_: (i, 0))
    return pl.pallas_call(
        ffn_kernel,
        grid_spec=pltpu.PrefetchScalarGridSpec(
            num_scalar_prefetch=1,
            grid=(ff // chunk,),
            in_specs=[
                full(t, d),
                full(t, d),
                pl.BlockSpec((1, d, chunk), lambda i, w: (w[0], 0, i)),
                pl.BlockSpec((1, chunk, d), lambda i, w: (w[0], i, 0)),
            ],
            out_specs=[full(t, d), full(t, d), piece, piece],
        ),
        out_shape=(
            jax.ShapeDtypeStruct((t, d), f32),
            jax.ShapeDtypeStruct((t, d), f32),
            jax.ShapeDtypeStruct((ff, d), bf16),
            jax.ShapeDtypeStruct((ff, d), bf16),
        ),
        compiler_params=params(),
        name="ffn_both",
    )(which, h2, cot, w_in, w_out)


def post_kernel(n_slots, ffn_ref, dh2_ref, resid_ref, cot_ref, slot_ref, mixed_ref, w_ref, gain_ref,
                out_ref, dres_ref, dmix_ref, gw_ref, gvec_ref):
    routed = slot_ref[...] < n_slots
    resid = resid_ref[...]
    ffn = jnp.where(routed, ffn_ref[...], 0.0).astype(bf16).astype(f32)
    out_ref[...] = (resid + ffn).astype(bf16)
    u = dh2_ref[...].astype(bf16).astype(f32)
    n, rstd = normalise(resid)
    d_resid = cot_ref[...].astype(f32) + norm_back(u, gain_ref[...], n, rstd)
    dres_ref[...] = d_resid
    d_branch = d_resid.astype(bf16)
    dmix_ref[...] = dot_nt(d_branch, w_ref[...]).astype(bf16)
    gw = dot_tn(mixed_ref[...], d_branch)
    gg = jnp.sum(u * n, axis=0, keepdims=True)
    gs = jnp.sum(u, axis=0, keepdims=True)

    @pl.when(pl.program_id(0) == 0)
    def _():
        gw_ref[...] = gw
        gvec_ref[0:1, :] = gg
        gvec_ref[1:2, :] = gs

    @pl.when(pl.program_id(0) > 0)
    def _():
        gw_ref[...] += gw
        gvec_ref[0:1, :] += gg
        gvec_ref[1:2, :] += gs


def post_ffn(ffn, dh2, resid, cotangent, slot_col, mixed, w_attn_out, gain, n_slots):
    t, d = resid.shape
    return pl.pallas_call(
        functools.partial(post_kernel, n_slots),
        grid=(t // ROWS,),
        in_specs=[rows_of(d)] * 4 + [rows_of(1), rows_of(d), full(d, d), full(1, d)],
        out_specs=[rows_of(d), rows_of(d), rows_of(d), full(d, d), full(2, d)],
        out_shape=(
            jax.ShapeDtypeStruct((t, d), bf16),
            jax.ShapeDtypeStruct((t, d), f32),
            jax.ShapeDtypeStruct((t, d), bf16),
            jax.ShapeDtypeStruct((d, d), f32),
            jax.ShapeDtypeStruct((2, d), f32),
        ),
        compiler_params=params(),
        name="post_ffn",
    )(ffn, dh2, resid, cotangent, slot_col, mixed, w_attn_out, gain)


def last_kernel(dq_ref, dk_ref, dv_ref, h1_ref, x_ref, dres_ref, w_ref, gain_ref,
                gtok_ref, gw_ref, gvec_ref):
    d = x_ref.shape[1]
    parts = (dq_ref[...], dk_ref[...], dv_ref[...])
    h1 = h1_ref[...]
    u = sum(dot_nt(p, w_ref[:, j * d:(j + 1) * d]) for j, p in enumerate(parts))
    n, rstd = normalise(x_ref[...].astype(f32))
    gtok_ref[...] = dres_ref[...] + norm_back(u, gain_ref[...], n, rstd)
    gg = jnp.sum(u * n, axis=0, keepdims=True)
    gs = jnp.sum(u, axis=0, keepdims=True)
    first = pl.program_id(0) == 0

    @pl.when(first)
    def _():
        for j, p in enumerate(parts):
            gw_ref[:, j * d:(j + 1) * d] = dot_tn(h1, p)
        gvec_ref[0:1, :] = gg
        gvec_ref[1:2, :] = gs

    @pl.when(jnp.logical_not(first))
    def _():
        for j, p in enumerate(parts):
            gw_ref[:, j * d:(j + 1) * d] += dot_tn(h1, p)
        gvec_ref[0:1, :] += gg
        gvec_ref[1:2, :] += gs


def last_step(dq, dk, dv, h1, tokens, d_resid, w_qkv, gain):
    t, d = tokens.shape
    return pl.pallas_call(
        last_kernel,
        grid=(t // ROWS,),
        in_specs=[rows_of(d)] * 6 + [full(d, 3 * d), full(1, d)],
        out_specs=[rows_of(d), full(d, 3 * d), full(2, d)],
        out_shape=(
            jax.ShapeDtypeStruct((t, d), f32),
            jax.ShapeDtypeStruct((d, 3 * d), f32),
            jax.ShapeDtypeStruct((2, d), f32),
        ),
        compiler_params=params(),
        name="last_step",
    )(dq, dk, dv, h1, tokens, d_resid, w_qkv, gain)


def shards(tokens, cotangent, seg_start, dispatch_slot, ln1_gain, ln1_shift, w_qkv, w_attn_out,
           ln2_gain, ln2_shift, w_in, w_out):
    tok_count = tokens.shape[0]
    n_expert = lax.axis_size("expert")
    group_size = n_expert // 2
    capacity = 2 * tok_count // n_expert
    n_slots = n_expert * capacity
    chunk = 384
    g1, s1, g2, s2 = (v[None] for v in (ln1_gain, ln1_shift, ln2_gain, ln2_shift))
    slot_col = dispatch_slot[:, None]
    modality = dispatch_slot // (capacity * group_size)
    language = jnp.max((modality == 1).astype(jnp.int32), keepdims=True)
    meta = block_meta(seg_start, 256, 512)
    seg_col = jnp.broadcast_to(seg_start[:, None], (tok_count, PAIR))
    seg_row = seg_start[None]

    h1, qkv = ln_qkv(tokens, g1, s1, w_qkv)
    mixed, lse = attn_fwd(qkv, meta, seg_col, seg_row)
    resid, h2, cotm = proj_ln(tokens, mixed, cotangent, slot_col, w_attn_out, g2, s2, n_slots)
    ffn, dh2, g_in, g_out = ffn_both(language, h2, cotm, w_in, w_out, chunk)
    own = (jnp.arange(2, dtype=jnp.int32) == language)[:, None, None]
    zero = jnp.zeros((), bf16)
    summed = [
        lax.psum(
            lax.psum_scatter(
                jnp.where(own, g[None], zero), "expert", scatter_dimension=1, tiled=True
            ),
            "dp",
        ).astype(f32)
        for g in (g_in, g_out)
    ]
    result_out, d_resid, d_mixed, g_wo, gvec2 = post_ffn(
        ffn, dh2, resid, cotangent, slot_col, mixed, w_attn_out, g2, n_slots
    )
    dq, dk, dv = attn_bwd(qkv, d_mixed, mixed, lse, meta, seg_col, seg_row)
    grad_tokens, g_wqkv, gvec1 = last_step(dq, dk, dv, h1, tokens, d_resid, w_qkv, g1)
    counts = jnp.sum(
        (modality[:, None] == jnp.arange(2, dtype=jnp.int32)[None]).astype(f32), axis=0
    )
    g_wqkv, g_wo = (
        v.astype(f32) for v in lax.psum((g_wqkv.astype(bf16), g_wo.astype(bf16)), ("dp", "expert"))
    )
    gvec1, gvec2, counts = lax.psum((gvec1, gvec2, counts), ("dp", "expert"))
    factor = (jnp.sum(counts) / (2.0 * counts))[:, None, None]
    grad_w_in = jnp.transpose(summed[0], (0, 2, 1)) * factor
    grad_w_out = summed[1] * factor
    return (
        result_out, grad_tokens, gvec1[0], gvec1[1], g_wqkv, g_wo, gvec2[0], gvec2[1],
        grad_w_in, grad_w_out, counts.astype(jnp.int32),
    )


def solution(mesh):
    rows = P(("dp", "expert"), None)
    flat = P(("dp", "expert"))
    rep = P()
    return jax.shard_map(
        shards,
        mesh=mesh,
        in_specs=(rows, rows, flat, flat) + (rep,) * 8,
        out_specs=(rows, rows) + (rep,) * 6 + (P(None, None, "expert"), P(None, "expert", None), rep),
        check_vma=False,
    )
```

time: 1360 us -> 511 us (0.38); the launches traced: 1350 us -> 518 us
  waiting for transfers between devices: 613 us -> 251 us
  matrix products: 352 us -> 0 us
  Pallas kernels: 0 us -> 165 us
  local copies, waits for them, and re-layouts: 147 us -> 11.2 us
  other arithmetic: 141 us -> 34.4 us
  starting transfers between devices: 30.5 us -> 0.35 us
    dot_general x26 -> x0, matrix products: 352 us -> none  [the longest x1 64.3 us: shards(): jnp.dot(flat_rows, expert_in, preferred_element_type=jnp.float32)]
    all_to_all x4 -> x0, waiting for transfers between devices: 278 us -> none  [the longest x1 107 us: shards(): lax.all_to_all(d_rows.reshape(n_expert, capacity, feat_width), 'expert',...]
    pallas_call x0 -> x7, Pallas kernels: none -> 165 us  [the longest x1 48.5 us: ffn_both(): pl.pallas_call(ffn_kernel, grid_spec=pltpu.PrefetchScalarGridSpec(num_sca...]
    reduce_scatter x2, waiting for transfers between devices: 215 us -> 139 us  [shards(): lax.psum_scatter(jnp.where(own, g[None], zero), 'expert', scatter_dimensi...]
    reduce_sum x10 -> x2, other arithmetic: 41.8 us -> 0.73 us  [the longest x1 0.6 us: shards(): factor = (jnp.sum(counts) / (2.0 * counts))[:, None, None]]
    gather x4 -> x0, local copies, waits for them, and re-layouts: 39.2 us -> none  [the longest x1 11.8 us: shards(): jnp.take(jnp.concatenate([normed_two_b, zero_row], axis=0), source_of, ax...]
    convert_element_type x7 -> x5, other arithmetic: 54 us -> 14.8 us  [the longest x2 7.15 us: shards(): v.astype(f32)]
    all_to_all x4 -> x0, starting transfers between devices: 30.4 us -> none  [the longest x1 8.73 us: shards(): lax.all_to_all(expert_rows_b, 'expert', split_axis=0, concat_axis=0, tile...]
  transfers between devices with their start and end apart: 8 -> 4, of which waited for: 7 -> 4; matrix products, arithmetic and copies ran while one was open for 29% -> 3% of each run, Pallas kernels for 0% -> 13%
where the time goes in v1:
time: 511 us; the launch traced here: 518 us
  waiting for transfers between devices  251 us (49%)
  Pallas kernels  165 us (32%)
  blocking collectives  39.5 us (8%)
  other arithmetic  34.4 us (7%)
  between operations  16.2 us (3%)
  local copies, waits for them, and re-layouts  11.2 us (2%)
    reduce_scatter x2, waiting for transfers between devices, shards(): lax.psum_scatter(jnp.where(own, g[None], zero), 'expert', scatter_dimensi...  139 us
    psum x1, waiting for transfers between devices, shards(): lax.psum(lax.psum_scatter(jnp.where(own, g[None], zero), 'expert', scatte...  70.5 us
    pallas_call x1, Pallas kernels, ffn_both(): pl.pallas_call(ffn_kernel, grid_spec=pltpu.PrefetchScalarGridSpec(num_sca...  48.5 us
    psum x1, waiting for transfers between devices, shards(): lax.psum((g_wqkv.astype(bf16), g_wo.astype(bf16)), ('dp', 'expert'))  41.4 us
    psum x1, blocking collectives, shards(): gvec1, gvec2, counts = lax.psum((gvec1, gvec2, counts), ('dp', 'expert'))  39.5 us
    pallas_call x1, Pallas kernels, attn_bwd(): pl.pallas_call(functools.partial(bwd_kernel, qb, win), out_shape=(sh, sh,...  36.6 us
    pallas_call x1, Pallas kernels, attn_fwd(): pl.pallas_call(functools.partial(fwd_kernel, qb, win), out_shape=(jax.Sha...  35.8 us
    pallas_call x1, Pallas kernels, last_step(): pl.pallas_call(last_kernel, grid=(t // ROWS,), in_specs=[rows_of(d)] * 6...  16.7 us
  transfers between devices with their start and end apart: 4, of which 4 were waited for; matrix products, arithmetic and copies ran while one was open for 3% of the time, Pallas kernels for 13%

profile of v1, /device:TPU:9, one launch (start us, length us, event | category | flops | bytes accessed | tf_op | source)
XLA Modules:
  0.0 518.3 jit_solution(15953429137580095711)
XLA Ops:
  8.0 0.0 reduce-scatter.3.cloned.1.call-start
  8.1 0.7 reshape.157
  8.8 0.2 fusion.5
  8.9 0.9 select_reduce_fusion.1
  9.9 0.7 fusion.4
  11.2 1.3 broadcast_in_dim.92.gain_ref
  12.4 1.3 broadcast_in_dim.93.shift_ref
  13.7 1.3 convert_reduce_fusion
  15.0 1.7 copy.27.slot_ref
  16.7 1.3 broadcast_in_dim.97.gain_ref
  18.0 1.3 broadcast_in_dim.98.shift_ref
  19.3 0.6 iota_compare_fusion
  19.9 0.1 pad.2.clone
  20.0 0.7 add_add_fusion.lo_ref
  20.7 0.0 copy-start.2
  20.7 8.5 %ln_qkv.1 = (bf16[1024,768]{1,0:T(8,128)(2,1)}, bf16[1024,2304]{1,0:T(8,128)(2,1)}) custom-call(bf16[1024,768]{1,0:T(8,128)(2,1)} %x_ref.5, f32[1,768]{1,0:T(1,128)} %broadcast_in_dim.92.gain_ref, f32[1,768]{1,0:T(1,128)} %broadcast_in_dim.93.shift_ref, bf16[768,2304]{1,0:T(8,128)(2,1)} %w_ref.7), custom_call_target="tpu_custom_call" | custom-call | tf_op jit(solution)/shard_map/ln_qkv/pallas_call | solution.py:277
  29.1 0.0 copy-done.2
  29.1 1.0 broadcast_in_dim.94.seg_col_ref
  30.2 35.8 %attn_fwd.1 = (bf16[1024,768]{1,0:T(8,128)(2,1)}, f32[6,2,1024]{2,1,0:T(2,128)}) custom-call(s32[3,4]{1,0:T(4,128)} %add_add_fusion.lo_ref, bf16[1024,2304]{1,0:T(8,128)(2,1)} %get-tuple-element.33.q_ref.k_ref.v_ref, bf16[1024,2304]{1,0:T(8,128)(2,1)} %get-tuple-element.33.q_ref.k_ref.v_ref, bf16[1024,2304]{1,0:T(8,128)(2,1)} %get-tuple-element.33.q_ref.k_ref.v_ref, ...), custom_call_target="tpu_custom_call" | custom-call | tf_op jit(solution)/shard_map/attn_fwd/pallas_call | solution.py:133
  66.0 7.0 %proj_ln.1 = (f32[1024,768]{1,0:T(8,128)}, bf16[1024,768]{1,0:T(8,128)(2,1)}, bf16[1024,768]{1,0:T(8,128)(2,1)}) custom-call(bf16[1024,768]{1,0:T(8,128)(2,1)} %x_ref.5, bf16[1024,768]{1,0:T(8,128)(2,1)} %get-tuple-element.34.mixed_ref.o_ref, bf16[1024,768]{1,0:T(8,128)(2,1)} %cot_ref.3, s32[1024,1]{1,0:T(8,128)} %copy.27.slot_ref, bf16[768,768]{1,0:T(8,128)(2,1)} %w_ref.6, ...), custom_call_target="tpu_custom_call" | custom-call | tf_op jit(solution)/shard_map/proj_ln/pallas_call | solution.py:303
  73.0 48.5 %ffn_both.1 = (f32[1024,768]{1,0:T(8,128)}, f32[1024,768]{1,0:T(8,128)}, bf16[3072,768]{1,0:T(8,128)(2,1)}, bf16[3072,768]{1,0:T(8,128)(2,1)}) custom-call(s32[1]{0:T(128)} %bitcast.which_ref, bf16[1024,768]{1,0:T(8,128)(2,1)} %get-tuple-element.35.h2_ref, bf16[1024,768]{1,0:T(8,128)(2,1)} %get-tuple-element.36.cot_ref, bf16[2,768,3072]{2,1,0:T(8,128)(2,1)} %win_ref.1, ...), custom_call_target="tpu_custom_call" | custom-call | tf_op jit(solution)/shard_map/ffn_both/pallas_call | solution.py:354
  121.4 11.0 %broadcast_select_fusion = (bf16[2,3072,768]{2,1,0:T(8,128)(2,1)}, bf16[2,3072,768]{2,1,0:T(8,128)(2,1)}) fusion(pred[2]{0:T(512)(128)(4,1)S(1)} %iota_compare_fusion, bf16[3072,768]{1,0:T(8,128)(2,1)} %get-tuple-element.54, bf16[3072,768]{1,0:T(8,128)(2,1)} %get-tuple-element.53), kind=kLoop, calls=%fused_computation | loop fusion | flops 9437184 | bytes 28311554 | tf_op jit(solution)/shard_map/jit(_where)/select_n | solution.py:495
  132.4 0.0 reduce-scatter.3.cloned.1.call-update
  132.4 0.0 reduce-scatter.5.cloned.1.call-start
  132.5 0.7 reduce-scatter.5.cloned.1.call-update
  133.2 0.2 all-reduce.6.cloned.1.call-start
  133.4 12.4 %post_ffn.1 = (bf16[1024,768]{1,0:T(8,128)(2,1)}, f32[1024,768]{1,0:T(8,128)}, bf16[1024,768]{1,0:T(8,128)(2,1)}, f32[768,768]{1,0:T(8,128)}, f32[2,768]{1,0:T(2,128)}) custom-call(f32[1024,768]{1,0:T(8,128)} %get-tuple-element.37.ffn_ref, f32[1024,768]{1,0:T(8,128)} %get-tuple-element.38.dh2_ref, f32[1024,768]{1,0:T(8,128)} %get-tuple-element.39.resid_ref, ...), custom_call_target="tpu_custom_call" | custom-call | tf_op jit(solution)/shard_map/post_ffn/pallas_call | solution.py:409
  145.8 36.6 %attn_bwd.1 = (bf16[1024,768]{1,0:T(8,128)(2,1)}, bf16[1024,768]{1,0:T(8,128)(2,1)}, bf16[1024,768]{1,0:T(8,128)(2,1)}) custom-call(s32[3,4]{1,0:T(4,128)} %add_add_fusion.lo_ref, bf16[1024,2304]{1,0:T(8,128)(2,1)} %get-tuple-element.33.q_ref.k_ref.v_ref, bf16[1024,2304]{1,0:T(8,128)(2,1)} %get-tuple-element.33.q_ref.k_ref.v_ref, ...), custom_call_target="tpu_custom_call" | custom-call | tf_op jit(solution)/shard_map/attn_bwd/pallas_call | solution.py:226
  182.4 16.7 %last_step.1 = (f32[1024,768]{1,0:T(8,128)}, f32[768,2304]{1,0:T(8,128)}, f32[2,768]{1,0:T(2,128)}) custom-call(bf16[1024,768]{1,0:T(8,128)(2,1)} %get-tuple-element.43.dq_ref, bf16[1024,768]{1,0:T(8,128)(2,1)} %get-tuple-element.44.dk_ref, bf16[1024,768]{1,0:T(8,128)(2,1)} %get-tuple-element.45.dv_ref, bf16[1024,768]{1,0:T(8,128)(2,1)} %get-tuple-element.46.h1_ref, ...), custom_call_target="tpu_custom_call" | custom-call | tf_op jit(solution)/shard_map/last_step/pallas_call | solution.py:455
  199.1 0.0 copy-start
  199.1 5.4 %convert_element_type.32 = bf16[768,2304]{1,0:T(8,128)(2,1)} convert(f32[768,2304]{1,0:T(8,128)} %get-tuple-element.50) | non-fusion elementwise | flops 1769472 | bytes 10616832 | tf_op jit(solution)/shard_map/convert_element_type | solution.py:510
  204.6 0.0 copy-done
  204.6 1.1 convert_element_type.34
  205.7 0.0 all-reduce.6.cloned.1.call-update
  205.7 0.0 copy-start.3
  205.7 0.0 copy-start.4
  205.7 0.0 all-reduce.8.cloned.1.call-start
  205.8 26.9 %reduce-scatter.3.cloned.1.call-done = bf16[2,384,768]{2,1,0:T(8,128)(2,1)} async-done(((bf16[2,3072,768]{2,1,0:T(8,128)(2,1)}), bf16[2,384,768]{2,1,0:T(8,128)(2,1)}) %reduce-scatter.3.cloned.1.call-update) | async-done | bytes 1179664 | tf_op jit(solution)/shard_map/reduce_scatter | solution.py:494
  232.7 111.6 %reduce-scatter.5.cloned.1.call-done = bf16[2,384,768]{2,1,0:T(8,128)(2,1)} async-done(((bf16[2,3072,768]{2,1,0:T(8,128)(2,1)}), bf16[2,384,768]{2,1,0:T(8,128)(2,1)}) %reduce-scatter.5.cloned.1.call-update) | async-done | bytes 1179664 | tf_op jit(solution)/shard_map/reduce_scatter | solution.py:494
  344.3 0.0 all-reduce.8.cloned.1.call-update
  344.3 0.1 fusion
  344.4 0.0 copy-done.3
  344.4 0.0 copy-done.4
  344.4 39.5 %all-reduce = (f32[2,768]{1,0:T(2,128)S(1)}, f32[2,768]{1,0:T(2,128)S(1)}, f32[2]{0:T(128)S(1)}) all-reduce(f32[2,768]{1,0:T(2,128)S(1)} %copy-done.4, f32[2,768]{1,0:T(2,128)S(1)} %copy-done.3, f32[2]{0:T(128)S(1)} %fusion), channel_id=1, replica_groups=mesh['dp'=4,'expert'=8] {'dp','expert'}, use_global_device_ids=true, to_apply=%region_6.7 | all-reduce | flops 3074 | bytes 24592 | tf_op jit(solution)/shard_map/psum | solution.py:512
  383.9 0.6 reduce_sum.19
  384.5 0.6 slice_reduce_fusion
  385.1 1.2 fusion.6
  386.3 41.4 %all-reduce.6.cloned.1.call-done = (bf16[768,2304]{1,0:T(8,128)(2,1)}, bf16[768,768]{1,0:T(8,128)(2,1)}) async-done(((bf16[768,2304]{1,0:T(8,128)(2,1)}, bf16[768,768]{1,0:T(8,128)(2,1)}), (bf16[768,2304]{1,0:T(8,128)(2,1)}, bf16[768,768]{1,0:T(8,128)(2,1)})) %all-reduce.6.cloned.1.call-update) | async-done | bytes 4718608 | tf_op jit(solution)/shard_map/psum | solution.py:510
  427.7 0.0 copy-start.1
  427.7 5.6 %convert_element_type.33 = f32[768,2304]{1,0:T(8,128)} convert(bf16[768,2304]{1,0:T(8,128)(2,1)} %get-tuple-element.99) | non-fusion elementwise | flops 1769472 | bytes 10616832 | tf_op jit(solution)/shard_map/convert_element_type | solution.py:510
  433.3 0.0 copy-done.1
  433.3 1.6 convert_element_type.35
  434.9 70.5 %all-reduce.8.cloned.1.call-done = (bf16[2,384,768]{2,1,0:T(8,128)(2,1)}, bf16[2,384,768]{2,1,0:T(8,128)(2,1)}) async-done(((bf16[2,384,768]{2,1,0:T(8,128)(2,1)}, bf16[2,384,768]{2,1,0:T(8,128)(2,1)}), (bf16[2,384,768]{2,1,0:T(8,128)(2,1)}, bf16[2,384,768]{2,1,0:T(8,128)(2,1)})) %all-reduce.8.cloned.1.call-update) | async-done | bytes 2359312 | tf_op jit(solution)/shard_map/psum | solution.py:493
  505.4 3.5 convert_multiply_fusion
  508.9 1.9 copy.29
  (2 shorter events, 0.0 us)
Async XLA Ops:
  8.0 224.7 %reduce-scatter.3.cloned.1.call-start = ((), (), s32[]{:S(2)}) async-start(), calls=%async_computation.2 | async-start | bytes 10616832 | tf_op jit(solution)/shard_map/reduce_scatter | solution.py:494
  20.7 8.5 %copy-start.2 = (s32[1024]{0:T(1024)S(1)}, s32[1024]{0:T(1024)}, u32[]{:S(2)}) copy-start(s32[1024]{0:T(1024)} %param.14) | copy-start | bytes 12292
  132.4 211.9 %reduce-scatter.5.cloned.1.call-start = ((), (), s32[]{:S(2)}) async-start(), calls=%async_computation.3 | async-start | bytes 10616832 | tf_op jit(solution)/shard_map/reduce_scatter | solution.py:494
  133.2 294.6 %all-reduce.6.cloned.1.call-start = ((), (), s32[]{:S(2)}) async-start(), calls=%async_computation.4 | async-start | bytes 9437184 | tf_op jit(solution)/shard_map/psum | solution.py:510
  199.1 5.4 %copy-start = (f32[768,768]{1,0:T(8,128)S(1)}, f32[768,768]{1,0:T(8,128)}, u32[]{:S(2)}) copy-start(f32[768,768]{1,0:T(8,128)} %get-tuple-element.51) | copy-start | bytes 7077892
  205.7 138.7 %copy-start.3 = (f32[2,768]{1,0:T(2,128)S(1)}, f32[2,768]{1,0:T(2,128)}, u32[]{:S(2)}) copy-start(f32[2,768]{1,0:T(2,128)} %get-tuple-element.52) | copy-start | bytes 18436
  205.7 138.7 %copy-start.4 = (f32[2,768]{1,0:T(2,128)S(1)}, f32[2,768]{1,0:T(2,128)}, u32[]{:S(2)}) copy-start(f32[2,768]{1,0:T(2,128)} %get-tuple-element.49) | copy-start | bytes 18436
  205.7 299.7 %all-reduce.8.cloned.1.call-start = ((), (), s32[]{:S(2)}) async-start(), calls=%async_computation.5 | async-start | bytes 4718592 | tf_op jit(solution)/shard_map/psum | solution.py:493
  427.7 5.6 %copy-start.1 = (bf16[768,768]{1,0:T(8,128)(2,1)S(1)}, bf16[768,768]{1,0:T(8,128)(2,1)}, u32[]{:S(2)}) copy-start(bf16[768,768]{1,0:T(8,128)(2,1)} %get-tuple-element.100) | copy-start | bytes 3538948
Sparse Core Ops, SparseCore 0:
  132.5 100.0 reduce-scatter.2
  235.1 109.1 reduce-scatter.4
Sparse Core Ops, SparseCore 1:
  205.8 221.9 all-reduce.5
  431.1 74.3 all-reduce.7
